TPU v7x, 256 devices: a whole 4x4x8 slice. The times are simulated.
256 devices in a mesh: sta: 64 (over z, x_lo, y), freq: 4 (over x_hi, core).
Axes of the slice: x: 4 (x_hi: 2, x_lo: 2; x = x_hi * 2 + x_lo), y: 4, z: 8, core: 2. Of those that a mesh axis runs over, the one named last changes fastest.
Arguments:
- spectra: bfloat16 [4, 2, 4096], P('freq', None, 'sta'), may hold values from -6 to 6
- green: bfloat16 [4, 2, 4096, 1024], P('freq', None, 'sta'), may hold values from -1.0546875 to 1.0546875
- source: float32 [4, 1024], P('freq'), may hold values from 0.25 to 4
- pair_mask: int32 [4096, 4096], P('sta'), may hold values 0 or 1
Outputs:
- new_source: float32 [4, 1024], P('freq')
- misfit: float32 [4], P('freq')
All inputs are finite; a program needn't handle non-finite values. No bound on the sum of `pair_mask` on one device may be relied on, other than what follows from the above.
Results may differ from a plain program's by a relative error of at most 0.0003.
Values may be sent and summed in bfloat16 or wider, within the bound.
No kernel may reach another device: no remote copies, remote signals or barrier semaphores. Data moves between devices by JAX's collectives and lax.ppermute only.
A program may use at most 64 MiB of HBM per device.

v0:
```python
import jax
import jax.numpy as jnp
from jax import lax
from jax.sharding import PartitionSpec as P


def copy_for_each(array, axis):
    peers = lax.axis_size(axis)
    return lax.all_to_all(
        jnp.broadcast_to(array[None], (peers, *array.shape)), axis, 0, 0, tiled=True
    )


def taken_together(array, axis):
    return copy_for_each(array, axis).sum(axis=0)


def in_one(arrays, axis):
    ends = [0]
    for a in arrays:
        ends.append(ends[-1] + a.size)
    total = taken_together(jnp.concatenate([a.ravel() for a in arrays]), axis)
    return tuple((total[b:e].reshape(a.shape) for a, b, e in zip(arrays, ends, ends[1:])))


def contract(a, b):
    return jnp.einsum("fix,fjx->fij", a, b, preferred_element_type=jnp.float32)


def spread(a, b):
    return jnp.einsum("fij,fjx->fix", a, b, preferred_element_type=jnp.float32)


def absorb(block_green, block_spec, weighted, spec_own, pair_mask):
    window = pair_mask.astype(jnp.float32)
    model_re = contract(weighted[:, 0], block_green[:, 0]) + contract(
        weighted[:, 1], block_green[:, 1]
    )
    model_im = contract(weighted[:, 1], block_green[:, 0]) - contract(
        weighted[:, 0], block_green[:, 1]
    )
    other = block_spec.astype(jnp.float32)
    data_re = (
        spec_own[:, 0, :, None] * other[:, 0, None, :]
        + spec_own[:, 1, :, None] * other[:, 1, None, :]
    )
    data_im = (
        spec_own[:, 1, :, None] * other[:, 0, None, :]
        - spec_own[:, 0, :, None] * other[:, 1, None, :]
    )
    resid_re = window[None] * (data_re - model_re)
    resid_im = window[None] * (data_im - model_im)
    mis = 0.5 * jnp.sum(resid_re * resid_re + resid_im * resid_im, axis=(1, 2))
    round_re = resid_re.astype(jnp.bfloat16)
    round_im = resid_im.astype(jnp.bfloat16)
    delta_re = spread(round_re, block_green[:, 0]) - spread(round_im, block_green[:, 1])
    delta_im = spread(round_re, block_green[:, 1]) + spread(round_im, block_green[:, 0])
    accum = jnp.stack([delta_re, delta_im], axis=1)
    return (accum, mis)


def local(spectra, green, source, pair_mask):
    count = lax.axis_size("sta")
    rows = green.shape[2]
    weighted = (source[:, None, None, :] * green).astype(jnp.bfloat16)
    spec_own = spectra.astype(jnp.float32)
    every_green, every_spec = (
        lax.all_gather(green, "sta", axis=2, tiled=True),
        lax.all_gather(spectra, "sta", axis=2, tiled=True),
    )
    state = absorb(every_green, every_spec, weighted, spec_own, pair_mask)
    accum, mis = state
    part = -jnp.sum(green * accum, axis=(1, 2))
    total_entries = green.shape[0] * lax.axis_size("freq") * green.shape[3]
    stations = rows * count
    grad, misfit = in_one((part, mis), "sta")
    squares = taken_together(jnp.sum(grad * grad), "freq")
    rms = jnp.sqrt(squares / total_entries + 1e-06)
    new_source = source * jnp.exp(-0.5 * grad / rms)
    return (new_source, misfit / (stations * stations))


def solution(mesh):
    placed = (P("freq", None, "sta"), P("freq", None, "sta", None), P("freq", None), P("sta", None))
    return jax.shard_map(
        local, mesh=mesh, in_specs=placed, out_specs=(P("freq", None), P("freq")), check_vma=False
    )
```

profile of v0, /device:TPU:1, one launch (start us, length us, event | category | flops | bytes accessed | tf_op | source)
XLA Modules:
  0.0 413.4 jit_solution(2978690009812199864)
XLA Ops:
  7.2 0.0 all-gather.2.cloned.1.call-start
  7.2 0.7 all-gather.2.cloned.1.call-update
  7.9 0.8 copy.9
  8.7 0.7 convert_element_type.26
  9.3 156.1 %all_gather.6 = bf16[1,2,4096]{1,0,2:T(2,128)(2,1)S(1)} all-gather(bf16[1,2,64]{1,0,2:T(2,128)(2,1)S(1)} %copy.9), channel_id=1, replica_groups=mesh['sta'=64,'freq'=4] {'sta'}, dimensions={2}, use_global_device_ids=true | all-gather | bytes 16640 | tf_op jit(solution)/shard_map/all_gather | solution.py:69
  165.4 2.2 convert_element_type.27
  167.6 1.0 fusion.18
  168.6 66.1 %slice_reduce_fusion.1 = (f32[4096]{0:T(1024)S(1)}, f32[4096]{0:T(1024)S(1)}) fusion(f32[1,2,4096]{1,0,2:T(1,128)S(1)} %convert_element_type.27), kind=kLoop, calls=%fused_computation.17 | loop fusion | bytes 65536 | tf_op jit(solution)/shard_map/slice | solution.py:44
  234.8 0.0 copy-start.2
  234.8 81.2 %all-gather.2.cloned.1.call-done = bf16[1,2,4096,1024]{3,2,1,0:T(8,128)(2,1)} async-done(((bf16[1,2,64,1024]{3,2,1,0:T(8,128)(2,1)}), bf16[1,2,4096,1024]{3,2,1,0:T(8,128)(2,1)}) %all-gather.2.cloned.1.call-update) | async-done | bytes 16777232 | tf_op jit(solution)/shard_map/all_gather | solution.py:68
  316.0 0.0 copy-start
  316.0 6.2 %fusion.3 = f32[64,4096]{1,0:T(8,128)S(1)} fusion(bf16[1,2,4096,1024]{3,2,1,0:T(8,128)(2,1)} %all-gather.2.cloned.1.call-done, bf16[1,2,64,1024]{3,2,1,0:T(8,128)(2,1)S(1)} %fusion.18), kind=kOutput, calls=%fused_computation.5 | convolution fusion | flops 536870912 | bytes 9568256 | tf_op jit(solution)/shard_map/fix,fjx->fij/dot_general | solution.py:27
  322.2 6.8 %fusion.1 = f32[64,4096]{1,0:T(8,128)S(1)} fusion(bf16[1,2,4096,1024]{3,2,1,0:T(8,128)(2,1)} %all-gather.2.cloned.1.call-done, bf16[1,2,64,1024]{3,2,1,0:T(8,128)(2,1)S(1)} %fusion.18), kind=kOutput, calls=%fused_computation.3 | convolution fusion | flops 536870912 | bytes 9568256 | tf_op jit(solution)/shard_map/fix,fjx->fij/dot_general | solution.py:27
  329.0 0.0 copy-done.2
  329.0 0.0 copy-done
  329.0 2.7 fusion.10
  331.7 1.6 fusion.2
  333.3 3.8 add_reduce_fusion
  337.0 1.6 fusion
  338.6 0.0 copy-start.1
  338.6 1.6 fusion.15
  340.2 0.0 copy-start.3
  340.2 1.6 fusion.17
  341.8 0.0 copy-done.1
  341.8 0.1 fusion.19
  342.6 0.2 broadcast_in_dim.4
  342.7 16.6 %all_to_all.12 = f32[64,1,1025]{2,1,0:T(1,128)S(1)} all-to-all(f32[64,1,1025]{2,1,0:T(1,128)S(1)} %broadcast_in_dim.4), channel_id=1, replica_groups=mesh['sta'=64,'freq'=4] {'sta'}, dimensions={0} | all-to-all | bytes 524800 | tf_op jit(solution)/shard_map/all_to_all | solution.py:9
  359.3 0.2 reduce_sum.47
  359.5 0.6 multiply_reduce_fusion
  360.1 0.6 slice.59
  360.7 1.2 broadcast_in_dim.5
  362.0 37.0 %all-to-all-start.1 = ((f32[4,1,1]{2,1,0:T(1,128)}), f32[4,1,1]{2,1,0:T(1,128)S(1)}, u32[]{:S(2)}, u32[]{:S(2)}) async-start(f32[4,1,1]{2,1,0:T(1,128)} %broadcast_in_dim.5), calls=%async_computation.1 | async-start | bytes 4096 | tf_op jit(solution)/shard_map/all_to_all | solution.py:9
  399.7 3.8 all-to-all-done.1
  403.5 0.6 reduce_sum.49
  404.8 0.0 copy-done.3
  404.8 0.6 mul.130
  (4 shorter events, 0.0 us)
Async XLA Ops:
  7.2 308.8 %all-gather.2.cloned.1.call-start = ((), (), s32[]{:S(2)}) async-start(), calls=%async_computation.2 | async-start | bytes 17039360 | tf_op jit(solution)/shard_map/all_gather | solution.py:68
  234.8 94.2 %copy-start.2 = (s32[64,4096]{1,0:T(8,128)S(1)}, s32[64,4096]{1,0:T(8,128)}, u32[]{:S(2)}) copy-start(s32[64,4096]{1,0:T(8,128)} %param.7) | copy-start | bytes 3145732
  316.0 13.0 %copy-start = (bf16[1,2,4096,1024]{3,2,1,0:T(8,128)(2,1)S(1)}, bf16[1,2,4096,1024]{3,2,1,0:T(8,128)(2,1)}, u32[]{:S(2)}) copy-start(bf16[1,2,4096,1024]{3,2,1,0:T(8,128)(2,1)} %all-gather.2.cloned.1.call-done) | copy-start | bytes 50331652
  338.6 3.2 copy-start.1
  340.2 64.6 %copy-start.3 = (f32[1,1024]{1,0:T(1,128)S(1)}, f32[1,1024]{1,0:T(1,128)}, u32[]{:S(2)}) copy-start(f32[1,1024]{1,0:T(1,128)} %param.6) | copy-start | bytes 12292
  362.0 41.5 %all-to-all-start.1 = ((f32[4,1,1]{2,1,0:T(1,128)}), f32[4,1,1]{2,1,0:T(1,128)S(1)}, u32[]{:S(2)}, u32[]{:S(2)}) async-start(f32[4,1,1]{2,1,0:T(1,128)} %broadcast_in_dim.5), calls=%async_computation.1 | async-start | bytes 4096 | tf_op jit(solution)/shard_map/all_to_all | solution.py:9
Sparse Core Ops, SparseCore 0:
  9.8 306.1 all-gather.1
where the time goes:
time: 414 us; the launch traced here: 413 us
  blocking collectives  173 us (42%)
  waiting for transfers between devices  85.7 us (21%)
  local copies, waits for them, and re-layouts  68.9 us (17%)
  starting transfers between devices  37.1 us (9%)
  matrix products  25.7 us (6%)
  between operations  17.4 us (4%)
  other arithmetic  5.96 us (1%)
    all_gather x1, blocking collectives, local(): lax.all_gather(spectra, 'sta', axis=2, tiled=True)  156 us
    all_gather x1, waiting for transfers between devices, local(): lax.all_gather(green, 'sta', axis=2, tiled=True)  81.2 us
    slice x1, local copies, waits for them, and re-layouts, absorb(): other[:, 0, None, :]  66.1 us
    all_to_all x1, starting transfers between devices, copy_for_each(): lax.all_to_all(jnp.broadcast_to(array[None], (peers, *array.shape)), axis...  37 us
    dot_general x4, matrix products, contract(): return jnp.einsum('fix,fjx->fij', a, b, preferred_element_type=jnp.float32)  19.4 us
    all_to_all x1, blocking collectives, copy_for_each(): lax.all_to_all(jnp.broadcast_to(array[None], (peers, *array.shape)), axis...  16.6 us
  transfers between devices with their start and end apart: 2, of which 2 were waited for; matrix products, arithmetic and copies ran while one was open for 17% of the time, Pallas kernels for 0%

commit v1 on v0

--- a/solution.py
+++ b/solution.py
@@ -65,7 +65,9 @@
     weighted = (source[:, None, None, :] * green).astype(jnp.bfloat16)
     spec_own = spectra.astype(jnp.float32)
     every_green, every_spec = (
-        lax.all_gather(green, "sta", axis=2, tiled=True),
+        jnp.concatenate(
+            lax.all_to_all(jnp.stack([green] * lax.axis_size("sta")), "sta", 0, 0), axis=2
+        ),
         lax.all_gather(spectra, "sta", axis=2, tiled=True),
     )
     state = absorb(every_green, every_spec, weighted, spec_own, pair_mask)

time: 414 us -> 682 us (1.65)
  blocking collectives: 173 us -> 521 us
  waiting for transfers between devices: 85.7 us -> 3.8 us
  local copies, waits for them, and re-layouts: 68.9 us -> 83.5 us
  between operations: 17.4 us -> 3.97 us
  starting transfers between devices: 37.1 us -> 46.7 us
  matrix products: 25.7 us -> 18 us
    all_gather x1, blocking collectives: 156 us -> 506 us  [local(): lax.all_gather(spectra, 'sta', axis=2, tiled=True)]
    all_gather x1 -> x0, waiting for transfers between devices: 81.2 us -> none  [local(): lax.all_gather(green, 'sta', axis=2, tiled=True)]
    all_to_all x0 -> x1, starting transfers between devices: none -> 14 us  [local(): lax.all_to_all(jnp.stack([green] * lax.axis_size('sta')), 'sta', 0, 0)]
    all_to_all x0 -> x1, local copies, waits for them, and re-layouts: none -> 8.76 us  [local(): lax.all_to_all(jnp.stack([green] * lax.axis_size('sta')), 'sta', 0, 0)]
    dot_general x4, matrix products: 19.4 us -> 11.8 us  [contract(): return jnp.einsum('fix,fjx->fij', a, b, preferred_element_type=jnp.float32)]
  transfers between devices with their start and end apart: 2 -> 2, of which waited for: 2 -> 1; matrix products, arithmetic and copies ran while one was open for 17% -> 10% of each run, Pallas kernels for 0% -> 0%
where the time goes in v1:
time: 682 us; the launch traced here: 681 us
  blocking collectives  521 us (76%)
  local copies, waits for them, and re-layouts  83.5 us (12%)
  starting transfers between devices  46.7 us (7%)
  matrix products  18 us (3%)
    all_gather x1, blocking collectives, local(): lax.all_gather(spectra, 'sta', axis=2, tiled=True)  506 us
    slice x1, local copies, waits for them, and re-layouts, absorb(): other[:, 0, None, :]  65.9 us
    all_to_all x1, starting transfers between devices, copy_for_each(): lax.all_to_all(jnp.broadcast_to(array[None], (peers, *array.shape)), axis...  32.7 us
    all_to_all x1, blocking collectives, copy_for_each(): lax.all_to_all(jnp.broadcast_to(array[None], (peers, *array.shape)), axis...  14.8 us
    all_to_all x1, starting transfers between devices, local(): lax.all_to_all(jnp.stack([green] * lax.axis_size('sta')), 'sta', 0, 0)  14 us
  transfers between devices with their start and end apart: 2, of which 1 were waited for; matrix products, arithmetic and copies ran while one was open for 10% of the time, Pallas kernels for 0%

profile of v1, /device:TPU:1, one launch (start us, length us, event | category | flops | bytes accessed | tf_op | source)
XLA Modules:
  0.0 681.2 jit_solution(8052288296891900131)
XLA Ops:
  0.6 6.7 stack.8
  7.3 0.0 copy-start.3
  7.3 0.0 copy-start
  7.3 0.0 copy-start.2
  7.3 14.0 %all-to-all-start = ((bf16[64,1,2,64,1024]{4,3,2,1,0:T(8,128)(2,1)}), bf16[64,1,2,64,1024]{4,3,2,1,0:T(8,128)(2,1)}, u32[]{:S(2)}, u32[]{:S(2)}) async-start(bf16[64,1,2,64,1024]{4,3,2,1,0:T(8,128)(2,1)} %stack.8), calls=%async_computation | async-start | bytes 33554432 | tf_op jit(solution)/shard_map/all_to_all | solution.py:69
  21.3 0.0 copy-done.3
  21.4 0.1 copy.12
  21.5 506.1 %all_gather.3 = bf16[1,2,4096]{1,0,2:T(2,128)(2,1)S(1)} all-gather(bf16[1,2,64]{1,0,2:T(2,128)(2,1)S(1)} %copy.12), channel_id=1, replica_groups=mesh['sta'=64,'freq'=4] {'sta'}, dimensions={2}, use_global_device_ids=true | all-gather | bytes 16640 | tf_op jit(solution)/shard_map/all_gather | solution.py:71
  527.6 2.2 convert_element_type.27
  529.8 0.0 copy-done
  529.8 0.0 copy-done.2
  529.8 65.9 %slice_reduce_fusion.1 = (f32[4096]{0:T(1024)S(1)}, f32[4096]{0:T(1024)S(1)}) fusion(f32[1,2,4096]{1,0,2:T(1,128)S(1)} %convert_element_type.27), kind=kLoop, calls=%fused_computation.17 | loop fusion | bytes 65536 | tf_op jit(solution)/shard_map/slice | solution.py:44
  595.8 0.0 all-to-all-done
  595.8 8.8 %copy.13 = bf16[64,1,2,64,1024]{4,3,0,2,1:T(8,128)(2,1)S(1)} copy(bf16[64,1,2,64,1024]{4,3,2,1,0:T(8,128)(2,1)} %all-to-all-done) | data formatting | bytes 33554432 | tf_op jit(solution)/shard_map/all_to_all | solution.py:69
  604.6 0.0 copy-start.1
  604.6 2.7 fusion.3
  607.2 2.7 fusion.1
  609.9 0.0 copy-done.1
  609.9 2.7 fusion.10
  612.6 1.6 fusion.2
  614.2 3.8 add_reduce_fusion
  617.9 1.6 fusion
  619.5 1.6 fusion.15
  621.1 1.6 fusion.17
  622.7 0.1 fusion.19
  623.4 0.2 broadcast_in_dim.4
  623.6 14.8 %all_to_all.17 = f32[64,1,1025]{2,1,0:T(1,128)S(1)} all-to-all(f32[64,1,1025]{2,1,0:T(1,128)S(1)} %broadcast_in_dim.4), channel_id=1, replica_groups=mesh['sta'=64,'freq'=4] {'sta'}, dimensions={0} | all-to-all | bytes 524800 | tf_op jit(solution)/shard_map/all_to_all | solution.py:9
  638.3 0.2 reduce_sum.47
  638.5 0.6 multiply_reduce_fusion
  639.1 0.6 slice.59
  639.7 1.2 broadcast_in_dim.5
  640.9 32.7 %all-to-all-start.2 = ((f32[4,1,1]{2,1,0:T(1,128)}), f32[4,1,1]{2,1,0:T(1,128)S(1)}, u32[]{:S(2)}, u32[]{:S(2)}) async-start(f32[4,1,1]{2,1,0:T(1,128)} %broadcast_in_dim.5), calls=%async_computation.2 | async-start | bytes 4096 | tf_op jit(solution)/shard_map/all_to_all | solution.py:9
  674.4 3.8 all-to-all-done.2
  678.2 0.6 reduce_sum.49
  679.5 0.6 mul.130
  (6 shorter events, 0.1 us)
Async XLA Ops:
  7.3 14.0 %copy-start.3 = (bf16[1,2,64]{2,1,0:T(2,128)(2,1)S(1)}, bf16[1,2,64]{2,1,0:T(2,128)(2,1)}, u32[]{:S(2)}) copy-start(bf16[1,2,64]{2,1,0:T(2,128)(2,1)} %param.4) | copy-start | bytes 772
  7.3 522.4 %copy-start = (bf16[1,2,64,1024]{3,2,1,0:T(8,128)(2,1)S(1)}, bf16[1,2,64,1024]{3,2,1,0:T(8,128)(2,1)}, u32[]{:S(2)}) copy-start(bf16[1,2,64,1024]{3,2,1,0:T(8,128)(2,1)} %param.5) | copy-start | bytes 786436
  7.3 522.4 %copy-start.2 = (f32[1,1024]{1,0:T(1,128)S(1)}, f32[1,1024]{1,0:T(1,128)}, u32[]{:S(2)}) copy-start(f32[1,1024]{1,0:T(1,128)} %param.6) | copy-start | bytes 12292
  7.3 588.4 %all-to-all-start = ((bf16[64,1,2,64,1024]{4,3,2,1,0:T(8,128)(2,1)}), bf16[64,1,2,64,1024]{4,3,2,1,0:T(8,128)(2,1)}, u32[]{:S(2)}, u32[]{:S(2)}) async-start(bf16[64,1,2,64,1024]{4,3,2,1,0:T(8,128)(2,1)} %stack.8), calls=%async_computation | async-start | bytes 33554432 | tf_op jit(solution)/shard_map/all_to_all | solution.py:69
  604.6 5.3 copy-start.1
  640.9 37.2 %all-to-all-start.2 = ((f32[4,1,1]{2,1,0:T(1,128)}), f32[4,1,1]{2,1,0:T(1,128)S(1)}, u32[]{:S(2)}, u32[]{:S(2)}) async-start(f32[4,1,1]{2,1,0:T(1,128)} %broadcast_in_dim.5), calls=%async_computation.2 | async-start | bytes 4096 | tf_op jit(solution)/shard_map/all_to_all | solution.py:9
